TPU v7x, 512 devices: a whole 4x8x8 slice. The times are simulated.
512 devices in a mesh: rows: 32 (over y_hi, z, core), cols: 16 (over y_lo, x).
Axes of the slice: x: 4, y: 8 (y_hi: 2, y_lo: 4; y = y_hi * 4 + y_lo), z: 8, core: 2. Of those that a mesh axis runs over, the one named last changes fastest.
Arguments:
- jac: bfloat16 [32768, 1024], P(('rows', 'cols')), may hold values from -0.29882812 to 0.29882812
- panel_jac: bfloat16 [32768, 512], P(('rows', 'cols')), may hold values from -6 to 6
- weights: float32 [32768], P(('rows', 'cols')), may hold values from 0.1 to 1
- tile_lists: int32 [1024, 4], P(('rows', 'cols')), may hold values from 0 to 95, as said below
- tile_masks: int32 [1024, 4], P(('rows', 'cols')), may hold values from 0 to 1
- tile_order: int32 [96], replicated, may hold values from 0 to 95, as said below
- factor_inverse: float32 [512, 512], replicated, as said below
Outputs:
- panel_factor: float32 [96, 256, 512], P('cols', 'rows')
Inputs may be any that keep to these rules, and one draw needn't show every extreme that they name: `tile_order`: a permutation of 0 to 95. `tile_lists`: the 4 tiles of one row block are distinct; among the active slots of one device's 2 row blocks, at most 2 name tiles whose positions i share i // 6; in every draw every device has 2 such slots for one and the same position range. `factor_inverse`: lower triangular with a positive diagonal.
All inputs are finite; a program needn't handle non-finite values.
Results may differ from a plain program's by a relative error of at most 0.0029.
Values may be sent and summed in bfloat16 or wider, within the bound.
A program may use at most 64 MiB of HBM per device.

v0:
```python
import jax
import jax.numpy as jnp
from jax import lax
from jax.sharding import PartitionSpec as P


def tile_positions(tile_lists, tile_order):
    tile_count = tile_order.shape[0]
    matches = tile_lists[:, :, None] == tile_order[None, None, :]
    return jnp.sum(jnp.where(matches, jnp.arange(tile_count, dtype=jnp.int32), 0), axis=2)


def apply_inverse(tiles, factor_inverse):
    return jnp.einsum("ntp,qp->ntq", tiles, factor_inverse, precision=lax.Precision.HIGHEST)


def local(jac, panel_jac, weights, tile_lists, tile_masks, tile_order, factor_inverse):
    block_count, slot_count = tile_lists.shape
    block_rows = jac.shape[0] // block_count
    tile_width = jac.shape[1] // slot_count
    panel_width = panel_jac.shape[1]
    owners = lax.axis_size("cols")
    per_owner = tile_order.shape[0] // owners
    positions = tile_positions(tile_lists, tile_order)
    weighted = (weights[:, None] * panel_jac).astype(jnp.bfloat16)
    first_place = lax.axis_index("cols") * per_owner
    jac_piece = lax.all_gather(jac, "cols", axis=0, tiled=True)
    weighted_piece = lax.all_gather(weighted, "cols", axis=0, tiled=True)
    place_piece = lax.all_gather(positions, "cols", axis=0, tiled=True)
    mask_piece = lax.all_gather(tile_masks, "cols", axis=0, tiled=True)
    blocks_here = place_piece.shape[0]
    local_place = place_piece - first_place
    chosen = (
        (local_place[:, :, None] == jnp.arange(per_owner, dtype=jnp.int32))
        & (mask_piece[:, :, None] == 1)
    ).astype(jnp.bfloat16)
    columns = jac_piece.reshape(blocks_here, block_rows, slot_count, tile_width)
    mixed_tiles = jnp.einsum(
        "bkn,brkt->brnt", chosen, columns, preferred_element_type=jnp.float32
    ).astype(jnp.bfloat16)
    panels = weighted_piece.reshape(blocks_here, block_rows, panel_width)
    gram_tiles = jnp.einsum(
        "brnt,brp->ntp", mixed_tiles, panels, preferred_element_type=jnp.float32
    )
    reduced = lax.psum_scatter(gram_tiles, "rows", scatter_dimension=1, tiled=True)
    return apply_inverse(reduced, factor_inverse)


def solution(mesh):
    in_specs = (
        P(("rows", "cols"), None),
        P(("rows", "cols"), None),
        P(("rows", "cols")),
        P(("rows", "cols"), None),
        P(("rows", "cols"), None),
        P(),
        P(),
    )
    out_specs = P("cols", "rows", None)
    return jax.shard_map(local, mesh=mesh, in_specs=in_specs, out_specs=out_specs, check_vma=False)
```

profile of v0, /device:TPU:4, one launch (start us, length us, event | category | flops | bytes accessed | tf_op | source)
XLA Modules:
  0.0 340.9 jit_solution(16019776710534135513)
XLA Ops:
  6.5 0.0 copy-start
  6.5 0.0 all-gather.5.cloned.1.call-start
  6.5 0.7 all-gather.5.cloned.1.call-update
  7.3 0.0 all-gather.7.cloned.1.call-start
  7.3 1.5 multiply_convert_fusion
  8.9 0.0 all-gather.7.cloned.1.call-update
  8.9 0.0 reduce-scatter.2.cloned.1.call-start
  8.9 37.9 %all-gather.1 = s32[16,2,4]{2,1,0:T(2,128)S(1)} all-gather(s32[1,2,4]{2,1,0:T(2,128)} %bitcast.27), channel_id=1, replica_groups=mesh['rows'=32,'cols'=16] {'cols'}, dimensions={0}, use_global_device_ids=true | all-gather | bytes 544 | tf_op jit(solution)/shard_map/all_gather | solution.py:30
  46.8 0.1 copy.18
  46.9 0.1 copy.24
  47.1 0.9 select_reduce_fusion
  48.0 38.3 %all-gather = s32[16,2,4]{2,1,0:T(2,128)S(1)} all-gather(s32[1,2,4]{2,1,0:T(2,128)S(1)} %bitcast.26), channel_id=1, replica_groups=mesh['rows'=32,'cols'=16] {'cols'}, dimensions={0}, use_global_device_ids=true | all-gather | bytes 544 | tf_op jit(solution)/shard_map/all_gather | solution.py:29
  86.3 9.3 %all-gather.5.cloned.1.call-done = bf16[1024,1024]{1,0:T(8,128)(2,1)} async-done(((bf16[64,1024]{1,0:T(8,128)(2,1)}), bf16[1024,1024]{1,0:T(8,128)(2,1)}) %all-gather.5.cloned.1.call-update) | async-done | bytes 2097168 | tf_op jit(solution)/shard_map/all_gather | solution.py:27
  95.6 3.3 reshape.12
  98.9 3.2 convert_bitcast_fusion
  102.2 77.8 %all-gather.7.cloned.1.call-done = bf16[1024,512]{1,0:T(8,128)(2,1)} async-done(((bf16[64,512]{1,0:T(8,128)(2,1)}), bf16[1024,512]{1,0:T(8,128)(2,1)}) %all-gather.7.cloned.1.call-update) | async-done | bytes 1048592 | tf_op jit(solution)/shard_map/all_gather | solution.py:28
  179.9 6.0 %fusion.2 = f32[6,256,512]{2,1,0:T(8,128)} fusion(bf16[32,32,512,1]{2,1,0,3:T(8,128)(2,1)} %bitcast.28, bf16[32,32,6,256]{3,2,1,0:T(8,128)(2,1)} %convert_bitcast_fusion), kind=kOutput, calls=%fused_computation.3 | convolution fusion | flops 1610612736 | bytes 7340032 | tf_op jit(solution)/shard_map/brnt,brp->ntp/dot_general | solution.py:42
  186.0 0.0 reduce-scatter.2.cloned.1.call-update
  186.0 145.7 %reduce-scatter.2.cloned.1.call-done = f32[6,8,512]{2,1,0:T(8,128)} async-done(((f32[6,256,512]{2,1,0:T(8,128)}), f32[6,8,512]{2,1,0:T(8,128)}) %reduce-scatter.2.cloned.1.call-update) | async-done | bytes 98320 | tf_op jit(solution)/shard_map/reduce_scatter | solution.py:45
  331.7 0.0 copy-done
  331.7 2.6 fusion.5
  (3 shorter events, 0.0 us)
Async XLA Ops:
  6.5 325.2 %copy-start = (f32[512,512]{1,0:T(8,128)S(1)}, f32[512,512]{1,0:T(8,128)}, u32[]{:S(2)}) copy-start(f32[512,512]{1,0:T(8,128)} %param.13) | copy-start | bytes 3145732
  6.5 89.1 %all-gather.5.cloned.1.call-start = ((), (), s32[]{:S(2)}) async-start(), calls=%async_computation.1 | async-start | bytes 2228224 | tf_op jit(solution)/shard_map/all_gather | solution.py:27
  7.3 172.7 %all-gather.7.cloned.1.call-start = ((), (), s32[]{:S(2)}) async-start(), calls=%async_computation.2 | async-start | bytes 1114112 | tf_op jit(solution)/shard_map/all_gather | solution.py:28
  8.9 322.8 %reduce-scatter.2.cloned.1.call-start = ((), (), s32[]{:S(2)}) async-start(), calls=%async_computation.3 | async-start | bytes 3244032 | tf_op jit(solution)/shard_map/reduce_scatter | solution.py:45
Sparse Core Ops, SparseCore 0:
  9.4 86.1 all-gather.4
  97.7 82.2 all-gather.6
  186.1 145.5 reduce-scatter.1
where the time goes:
time: 341 us
  waiting for transfers between devices  234 us (69%)
  blocking collectives  76.2 us (22%)
  between operations  13.1 us (4%)
  matrix products  11.9 us (3%)
  local copies, waits for them, and re-layouts  3.56 us (1%)
    reduce_scatter x1, waiting for transfers between devices, local(): lax.psum_scatter(gram_tiles, 'rows', scatter_dimension=1, tiled=True)  146 us
    all_gather x1, waiting for transfers between devices, local(): weighted_piece = lax.all_gather(weighted, 'cols', axis=0, tiled=True)  77.8 us
    all_gather x1, blocking collectives, local(): place_piece = lax.all_gather(positions, 'cols', axis=0, tiled=True)  38.3 us
    all_gather x1, blocking collectives, local(): mask_piece = lax.all_gather(tile_masks, 'cols', axis=0, tiled=True)  37.9 us
    all_gather x1, waiting for transfers between devices, local(): jac_piece = lax.all_gather(jac, 'cols', axis=0, tiled=True)  9.29 us
  transfers between devices with their start and end apart: 3, of which 3 were waited for; matrix products, arithmetic and copies ran while one was open for 3% of the time, Pallas kernels for 0%

commit v1 on v0

--- a/solution.py
+++ b/solution.py
@@ -27,7 +27,9 @@
     jac_piece = lax.all_gather(jac, "cols", axis=0, tiled=True)
     weighted_piece = lax.all_gather(weighted, "cols", axis=0, tiled=True)
     place_piece = lax.all_gather(positions, "cols", axis=0, tiled=True)
-    mask_piece = lax.all_gather(tile_masks, "cols", axis=0, tiled=True)
+    mask_piece = jnp.concatenate(
+        lax.all_to_all(jnp.stack([tile_masks] * lax.axis_size("cols")), "cols", 0, 0), axis=0
+    )
     blocks_here = place_piece.shape[0]
     local_place = place_piece - first_place
     chosen = (

time: 341 us -> 341 us (level)
  the two profiles are of different devices: /device:TPU:4 before, /device:TPU:2 now
where the time goes in v1:
time: 341 us
  waiting for transfers between devices  262 us (77%)
  blocking collectives  37.7 us (11%)
  between operations  13.1 us (4%)
  matrix products  11.9 us (3%)
  starting transfers between devices  9.25 us (3%)
  local copies, waits for them, and re-layouts  4.84 us (1%)
    reduce_scatter x1, waiting for transfers between devices, local(): lax.psum_scatter(gram_tiles, 'rows', scatter_dimension=1, tiled=True)  142 us
    all_gather x1, waiting for transfers between devices, local(): weighted_piece = lax.all_gather(weighted, 'cols', axis=0, tiled=True)  78 us
    all_gather x1, waiting for transfers between devices, local(): jac_piece = lax.all_gather(jac, 'cols', axis=0, tiled=True)  41.1 us
    all_gather x1, blocking collectives, local(): place_piece = lax.all_gather(positions, 'cols', axis=0, tiled=True)  37.7 us
    all_to_all x1, starting transfers between devices, local(): lax.all_to_all(jnp.stack([tile_masks] * lax.axis_size('cols')), 'cols', 0...  9.17 us
  transfers between devices with their start and end apart: 4, of which 3 were waited for; matrix products, arithmetic and copies ran while one was open for 3% of the time, Pallas kernels for 0%

profile of v1, /device:TPU:2, one launch (start us, length us, event | category | flops | bytes accessed | tf_op | source)
XLA Modules:
  0.0 340.8 jit_solution(5485587060489413828)
XLA Ops:
  6.5 0.0 copy-start
  6.5 0.0 all-gather.4.cloned.1.call-start
  6.5 0.7 all-gather.4.cloned.1.call-update
  7.3 0.0 all-gather.6.cloned.1.call-start
  7.3 1.5 multiply_convert_fusion
  8.9 0.0 all-gather.6.cloned.1.call-update
  8.9 1.3 stack.2
  10.2 9.2 %all-to-all-start = ((s32[16,2,4]{2,1,0:T(2,128)}), s32[16,2,4]{2,1,0:T(2,128)S(1)}, u32[]{:S(2)}, u32[]{:S(2)}) async-start(s32[16,2,4]{2,1,0:T(2,128)} %stack.2), calls=%async_computation | async-start | bytes 32768 | tf_op jit(solution)/shard_map/all_to_all | solution.py:31
  19.3 0.0 reduce-scatter.2.cloned.1.call-start
  19.4 0.9 select_reduce_fusion
  20.3 37.7 %all-gather = s32[16,2,4]{2,1,0:T(2,128)S(1)} all-gather(s32[1,2,4]{2,1,0:T(2,128)S(1)} %bitcast.25), channel_id=1, replica_groups=mesh['rows'=32,'cols'=16] {'cols'}, dimensions={0}, use_global_device_ids=true | all-gather | bytes 544 | tf_op jit(solution)/shard_map/all_gather | solution.py:29
  58.0 0.0 all-to-all-done
  58.0 0.1 copy.18
  58.1 0.1 copy.24
  58.2 41.1 %all-gather.4.cloned.1.call-done = bf16[1024,1024]{1,0:T(8,128)(2,1)} async-done(((bf16[64,1024]{1,0:T(8,128)(2,1)}), bf16[1024,1024]{1,0:T(8,128)(2,1)}) %all-gather.4.cloned.1.call-update) | async-done | bytes 2097168 | tf_op jit(solution)/shard_map/all_gather | solution.py:27
  99.3 3.3 reshape.21
  102.7 3.2 convert_bitcast_fusion
  105.9 78.0 %all-gather.6.cloned.1.call-done = bf16[1024,512]{1,0:T(8,128)(2,1)} async-done(((bf16[64,512]{1,0:T(8,128)(2,1)}), bf16[1024,512]{1,0:T(8,128)(2,1)}) %all-gather.6.cloned.1.call-update) | async-done | bytes 1048592 | tf_op jit(solution)/shard_map/all_gather | solution.py:28
  183.9 6.0 %fusion.2 = f32[6,256,512]{2,1,0:T(8,128)} fusion(bf16[32,32,512,1]{2,1,0,3:T(8,128)(2,1)} %bitcast.26, bf16[32,32,6,256]{3,2,1,0:T(8,128)(2,1)} %convert_bitcast_fusion), kind=kOutput, calls=%fused_computation.3 | convolution fusion | flops 1610612736 | bytes 7340032 | tf_op jit(solution)/shard_map/brnt,brp->ntp/dot_general | solution.py:44
  189.9 0.0 reduce-scatter.2.cloned.1.call-update
  189.9 141.7 %reduce-scatter.2.cloned.1.call-done = f32[6,8,512]{2,1,0:T(8,128)} async-done(((f32[6,256,512]{2,1,0:T(8,128)}), f32[6,8,512]{2,1,0:T(8,128)}) %reduce-scatter.2.cloned.1.call-update) | async-done | bytes 98320 | tf_op jit(solution)/shard_map/reduce_scatter | solution.py:47
  331.7 0.0 copy-done
  331.7 2.6 fusion.5
  (3 shorter events, 0.0 us)
Async XLA Ops:
  6.5 325.1 %copy-start = (f32[512,512]{1,0:T(8,128)S(1)}, f32[512,512]{1,0:T(8,128)}, u32[]{:S(2)}) copy-start(f32[512,512]{1,0:T(8,128)} %param.13) | copy-start | bytes 3145732
  6.5 92.8 %all-gather.4.cloned.1.call-start = ((), (), s32[]{:S(2)}) async-start(), calls=%async_computation.2 | async-start | bytes 2228224 | tf_op jit(solution)/shard_map/all_gather | solution.py:27
  7.3 176.6 %all-gather.6.cloned.1.call-start = ((), (), s32[]{:S(2)}) async-start(), calls=%async_computation.3 | async-start | bytes 1114112 | tf_op jit(solution)/shard_map/all_gather | solution.py:28
  10.2 47.8 %all-to-all-start = ((s32[16,2,4]{2,1,0:T(2,128)}), s32[16,2,4]{2,1,0:T(2,128)S(1)}, u32[]{:S(2)}, u32[]{:S(2)}) async-start(s32[16,2,4]{2,1,0:T(2,128)} %stack.2), calls=%async_computation | async-start | bytes 32768 | tf_op jit(solution)/shard_map/all_to_all | solution.py:31
  19.3 312.3 %reduce-scatter.2.cloned.1.call-start = ((), (), s32[]{:S(2)}) async-start(), calls=%async_computation.4 | async-start | bytes 3244032 | tf_op jit(solution)/shard_map/reduce_scatter | solution.py:47
Sparse Core Ops, SparseCore 0:
  9.4 89.8 all-gather.3
  101.4 82.3 all-gather.5
  190.0 141.5 reduce-scatter.1

commit v2 on v0

--- a/solution.py
+++ b/solution.py
@@ -24,8 +24,11 @@
     positions = tile_positions(tile_lists, tile_order)
     weighted = (weights[:, None] * panel_jac).astype(jnp.bfloat16)
     first_place = lax.axis_index("cols") * per_owner
-    jac_piece = lax.all_gather(jac, "cols", axis=0, tiled=True)
-    weighted_piece = lax.all_gather(weighted, "cols", axis=0, tiled=True)
+    jac_piece, weighted_piece = jnp.split(
+        lax.all_gather(jnp.concatenate([jac, weighted], axis=1), "cols", axis=0, tiled=True),
+        [jac.shape[1]],
+        axis=1,
+    )
     place_piece = lax.all_gather(positions, "cols", axis=0, tiled=True)
     mask_piece = lax.all_gather(tile_masks, "cols", axis=0, tiled=True)
     blocks_here = place_piece.shape[0]

time: 341 us -> 265 us (0.78)
  the two profiles are of different devices: /device:TPU:4 before, /device:TPU:2 now
where the time goes in v2:
time: 265 us
  waiting for transfers between devices  154 us (58%)
  blocking collectives  80 us (30%)
  between operations  13.4 us (5%)
  matrix products  9.72 us (4%)
  local copies, waits for them, and re-layouts  4.58 us (2%)
  other arithmetic  3.51 us (1%)
    reduce_scatter x1, waiting for transfers between devices, local(): lax.psum_scatter(gram_tiles, 'rows', scatter_dimension=1, tiled=True)  142 us
    all_gather x1, blocking collectives, local(): mask_piece = lax.all_gather(tile_masks, 'cols', axis=0, tiled=True)  42.9 us
    all_gather x1, blocking collectives, local(): place_piece = lax.all_gather(positions, 'cols', axis=0, tiled=True)  37.2 us
    all_gather x1, waiting for transfers between devices, local(): lax.all_gather(jnp.concatenate([jac, weighted], axis=1), 'cols', axis=0,...  12.2 us
  transfers between devices with their start and end apart: 2, of which 2 were waited for; matrix products, arithmetic and copies ran while one was open for 0% of the time, Pallas kernels for 0%

profile of v2, /device:TPU:2, one launch (start us, length us, event | category | flops | bytes accessed | tf_op | source)
XLA Modules:
  0.0 265.1 jit_solution(6126125571972361424)
XLA Ops:
  6.5 0.0 copy-start
  6.5 0.0 all-gather.4.cloned.1.call-start
  6.5 1.0 multiply_convert_fusion
  7.6 1.6 pad_maximum_fusion
  9.1 0.0 all-gather.4.cloned.1.call-update
  9.2 0.0 reduce-scatter.2.cloned.1.call-start
  9.2 42.9 %all-gather.1 = s32[16,2,4]{2,1,0:T(2,128)S(1)} all-gather(s32[1,2,4]{2,1,0:T(2,128)} %bitcast.28), channel_id=1, replica_groups=mesh['rows'=32,'cols'=16] {'cols'}, dimensions={0}, use_global_device_ids=true | all-gather | bytes 544 | tf_op jit(solution)/shard_map/all_gather | solution.py:33
  52.1 0.1 copy.18
  52.2 0.1 copy.24
  52.3 0.9 select_reduce_fusion
  53.2 37.2 %all-gather = s32[16,2,4]{2,1,0:T(2,128)S(1)} all-gather(s32[1,2,4]{2,1,0:T(2,128)S(1)} %bitcast.27), channel_id=1, replica_groups=mesh['rows'=32,'cols'=16] {'cols'}, dimensions={0}, use_global_device_ids=true | all-gather | bytes 544 | tf_op jit(solution)/shard_map/all_gather | solution.py:32
  90.4 12.2 %all-gather.4.cloned.1.call-done = bf16[1024,1536]{1,0:T(8,128)(2,1)} async-done(((bf16[64,1536]{1,0:T(8,128)(2,1)}), bf16[1024,1536]{1,0:T(8,128)(2,1)}) %all-gather.4.cloned.1.call-update) | async-done | bytes 3145744 | tf_op jit(solution)/shard_map/all_gather | solution.py:28
  102.6 0.0 slice-start
  102.6 1.6 slice-done
  104.2 2.8 %reshape.12 = bf16[32,32,4,256]{3,2,1,0:T(4,128)(2,1)} reshape(bf16[1024,1024]{1,0:T(8,128)(2,1)S(1)} %slice-done) | data formatting | bytes 4194304 | tf_op jit(solution)/shard_map/reshape | solution.py:40
  106.9 0.0 slice-start.1
  106.9 3.6 %convert_bitcast_fusion = bf16[32,32,6,256]{3,2,1,0:T(8,128)(2,1)S(1)} fusion(bf16[32,32,4,256]{3,2,1,0:T(4,128)(2,1)} %reshape.12, s32[32,4]{1,0:T(8,128)S(1)} %bitcast.25, pred[32,4]{1,0:T(8,128)(4,1)S(1)} %reshape.26), kind=kOutput, calls=%fused_computation | convolution fusion | flops 14157312 | bytes 5243520 | tf_op jit(solution)/shard_map/bkn,brkt->brnt/dot_general | solution.py:41
  110.5 0.0 slice-done.1
  110.5 3.5 %fusion.2 = f32[6,256,512]{2,1,0:T(8,128)} fusion(bf16[32,32,512,1]{2,1,0,3:T(8,128)(2,1)S(1)} %bitcast.24, bf16[32,32,6,256]{3,2,1,0:T(8,128)(2,1)S(1)} %convert_bitcast_fusion), kind=kOutput, calls=%fused_computation.3 | convolution fusion | flops 1610612736 | bytes 7340032 | tf_op jit(solution)/shard_map/brnt,brp->ntp/dot_general | solution.py:45
  114.1 0.0 reduce-scatter.2.cloned.1.call-update
  114.1 141.6 %reduce-scatter.2.cloned.1.call-done = f32[6,8,512]{2,1,0:T(8,128)} async-done(((f32[6,256,512]{2,1,0:T(8,128)}), f32[6,8,512]{2,1,0:T(8,128)}) %reduce-scatter.2.cloned.1.call-update) | async-done | bytes 98320 | tf_op jit(solution)/shard_map/reduce_scatter | solution.py:48
  255.7 0.0 copy-done
  255.7 2.6 fusion.5
  (3 shorter events, 0.0 us)
Async XLA Ops:
  6.5 249.1 %copy-start = (f32[512,512]{1,0:T(8,128)S(1)}, f32[512,512]{1,0:T(8,128)}, u32[]{:S(2)}) copy-start(f32[512,512]{1,0:T(8,128)} %param.13) | copy-start | bytes 3145732
  6.5 96.0 %all-gather.4.cloned.1.call-start = ((), (), s32[]{:S(2)}) async-start(), calls=%async_computation.1 | async-start | bytes 3342336 | tf_op jit(solution)/shard_map/all_gather | solution.py:28
  9.2 246.5 %reduce-scatter.2.cloned.1.call-start = ((), (), s32[]{:S(2)}) async-start(), calls=%async_computation.2 | async-start | bytes 3244032 | tf_op jit(solution)/shard_map/reduce_scatter | solution.py:48
  102.6 1.6 slice-start
  106.9 3.6 %slice-start.1 = ((bf16[1024,1536]{1,0:T(8,128)(2,1)}), bf16[1024,512]{1,0:T(8,128)(2,1)S(1)}, s32[]{:S(2)}) async-start(bf16[1024,1536]{1,0:T(8,128)(2,1)} %all-gather.4.cloned.1.call-done), calls=%async_computation.4 | async-start | bytes 2097152 | tf_op jit(solution)/shard_map/split | solution.py:27
Sparse Core Ops, SparseCore 0:
  9.4 93.1 all-gather.3
  114.2 141.4 reduce-scatter.1
